TPU v7x, 32 devices: a whole 2x2x4 slice. The times are simulated.
32 devices in a mesh: dp: 4 (over y, x), expert: 8 (over z, core).
Axes of the slice: x: 2, y: 2, z: 4, core: 2. Of those that a mesh axis runs over, the one named last changes fastest.
Arguments:
- tokens: bfloat16 [2048, 4096], P(('dp', 'expert')), may hold values from -6 to 6
- grads_out: bfloat16 [2048, 4096], P(('dp', 'expert')), may hold values from -6 to 6
- routes: int32 [2048, 2], P(('dp', 'expert')), may hold values from 0 to 31, all different within a row; in each aligned block of 64 rows (0 to 63, 64 to 127, ...) at most 4 rows name the same one
- route_weights: float32 [2048, 2], P(('dp', 'expert')), may hold values from 0.2 to 1
- depth_filter: float32 [32, 5, 512], P('expert'), may hold values from -2.5 to 2.5
- point_weight: bfloat16 [512, 32, 1024], P('dp', 'expert'), may hold values from -0.25 to 0.25
Outputs:
- mixed: bfloat16 [2048, 4096], P(('dp', 'expert'))
- token_grads: bfloat16 [2048, 4096], P(('dp', 'expert'))
- point_grads: float32 [512, 32, 1024], P('dp', 'expert')
- depth_grads: float32 [32, 5, 512], P('expert')
Inputs may be any that keep to these rules, and one draw needn't show every extreme that they name: `routes`: the two experts of a frame differ; among the 64 frames of one device no expert is named more than 4 times.
All inputs are finite; a program needn't handle non-finite values.
Results may differ from a plain program's by a relative error of at most 0.0095.
Values may be sent and summed in bfloat16 or wider, within the bound.
No kernel may reach another device: no remote copies, remote signals or barrier semaphores. Data moves between devices by JAX's collectives and lax.ppermute only.
A program may use at most 64 MiB of HBM per device.

v0:
```python
import jax
import jax.numpy as jnp
from jax import lax
from jax.sharding import PartitionSpec as P

KERNEL_TAPS = 5
DILATION_STEP = 2
CAP = 4


def shifted_input(field, tap_offset):
    width = field.shape[-2]
    pads = [(0, 0)] * (field.ndim - 2) + [(abs(tap_offset), abs(tap_offset)), (0, 0)]
    padded = jnp.pad(field, pads)
    begin = abs(tap_offset) + tap_offset
    return lax.slice_in_dim(padded, begin, begin + width, axis=field.ndim - 2)


def shards(tokens, grads_out, routes, route_weights, depth_filter, point_weight):
    tok_count = tokens.shape[0]
    dev_count = lax.axis_size("expert")
    exp_local = depth_filter.shape[0]
    exp_total = exp_local * dev_count
    slot_count = 2 * tok_count
    frame_width = tokens.shape[1]
    channels = point_weight.shape[2] // 2
    bins = frame_width // channels
    route_flat = routes.reshape(slot_count)
    onehot = (route_flat[:, None] == jnp.arange(exp_total, dtype=jnp.int32)[None, :]).astype(
        jnp.int32
    )
    ranks = jnp.sum((jnp.cumsum(onehot, axis=0) - 1) * onehot, axis=1)
    slot_ids = route_flat * CAP + ranks
    placing = (slot_ids[None, :] == jnp.arange(exp_total * CAP, dtype=jnp.int32)[:, None]).astype(
        jnp.bfloat16
    )
    tokens_twice = jnp.repeat(tokens, 2, axis=0)
    cotan_twice = (
        route_weights.reshape(slot_count, 1) * jnp.repeat(grads_out, 2, axis=0).astype(jnp.float32)
    ).astype(jnp.bfloat16)
    send_frames = jnp.dot(placing, tokens_twice, preferred_element_type=jnp.float32).astype(
        jnp.bfloat16
    )
    send_cotan = jnp.dot(placing, cotan_twice, preferred_element_type=jnp.float32).astype(
        jnp.bfloat16
    )
    send_frames = send_frames.reshape(dev_count, exp_local * CAP, frame_width)
    send_cotan = send_cotan.reshape(dev_count, exp_local * CAP, frame_width)

    def to_local(buffer):
        shaped = buffer.reshape(dev_count, exp_local, CAP, bins, channels)
        return jnp.transpose(shaped, (1, 0, 2, 3, 4)).reshape(
            exp_local, dev_count * CAP, bins, channels
        )

    def to_source(buffer):
        shaped = buffer.reshape(exp_local, dev_count, CAP, frame_width)
        return jnp.transpose(shaped, (1, 0, 2, 3)).reshape(dev_count, exp_local * CAP, frame_width)

    recv_frames, recv_cotan = (
        lax.all_to_all(send_frames, "expert", split_axis=0, concat_axis=0, tiled=True),
        lax.all_to_all(send_cotan, "expert", split_axis=0, concat_axis=0, tiled=True),
    )
    input_frames = to_local(recv_frames).astype(jnp.float32)
    hidden_state = jnp.zeros(input_frames.shape, jnp.float32)
    for tap_index in range(KERNEL_TAPS):
        hidden_state = hidden_state + depth_filter[:, tap_index][:, None, None, :] * shifted_input(
            input_frames, DILATION_STEP * (tap_index - KERNEL_TAPS // 2)
        )
    hidden_state = hidden_state.astype(jnp.bfloat16)
    full_filter = lax.all_gather(point_weight, "dp", axis=0, tiled=True)
    preact = jnp.einsum(
        "erpc,ceo->erpo", hidden_state, full_filter, preferred_element_type=jnp.float32
    )
    value_half = preact[..., :channels]
    gate_sig = jax.nn.sigmoid(preact[..., channels:])
    expert_out = (value_half * gate_sig).astype(jnp.bfloat16)
    cotan = to_local(recv_cotan).astype(jnp.float32)
    dpre = jnp.concatenate(
        [cotan * gate_sig, cotan * value_half * gate_sig * (1.0 - gate_sig)], axis=-1
    ).astype(jnp.bfloat16)
    dhidden = jnp.einsum("erpo,ceo->erpc", dpre, full_filter, preferred_element_type=jnp.float32)
    frame_grad = jnp.zeros(input_frames.shape, jnp.float32)
    tap_grads = []
    for tap_index in range(KERNEL_TAPS):
        tap_offset = DILATION_STEP * (tap_index - KERNEL_TAPS // 2)
        frame_grad = frame_grad + depth_filter[:, tap_index][:, None, None, :] * shifted_input(
            dhidden, -tap_offset
        )
        tap_grads.append(jnp.sum(dhidden * shifted_input(input_frames, tap_offset), axis=(1, 2)))
    frame_grad = frame_grad.astype(jnp.bfloat16)
    depth_grads = lax.psum(jnp.stack(tap_grads, axis=1).astype(jnp.bfloat16), "dp").astype(
        jnp.float32
    )
    point_grads = lax.psum_scatter(
        jnp.einsum("erpc,erpo->ceo", hidden_state, dpre, preferred_element_type=jnp.float32).astype(
            jnp.bfloat16
        ),
        "dp",
        scatter_dimension=0,
        tiled=True,
    ).astype(jnp.float32)
    back_out, back_grad = (
        lax.all_to_all(to_source(expert_out), "expert", split_axis=0, concat_axis=0, tiled=True),
        lax.all_to_all(to_source(frame_grad), "expert", split_axis=0, concat_axis=0, tiled=True),
    )
    back_out = back_out.reshape(exp_total * CAP, frame_width)
    back_grad = back_grad.reshape(exp_total * CAP, frame_width)
    slot_out = jnp.dot(placing.T, back_out, preferred_element_type=jnp.float32).reshape(
        tok_count, 2, frame_width
    )
    slot_grad = jnp.dot(placing.T, back_grad, preferred_element_type=jnp.float32).reshape(
        tok_count, 2, frame_width
    )
    mixed = jnp.sum(route_weights[:, :, None] * slot_out, axis=1).astype(jnp.bfloat16)
    token_grads = jnp.sum(slot_grad, axis=1).astype(jnp.bfloat16)
    return (mixed, token_grads, point_grads, depth_grads)


def solution(mesh):
    placed = (
        P(("dp", "expert"), None),
        P(("dp", "expert"), None),
        P(("dp", "expert"), None),
        P(("dp", "expert"), None),
        P("expert", None, None),
        P("dp", "expert", None),
    )
    return jax.shard_map(
        shards,
        mesh=mesh,
        in_specs=placed,
        out_specs=(
            P(("dp", "expert"), None),
            P(("dp", "expert"), None),
            P("dp", "expert", None),
            P("expert", None, None),
        ),
        check_vma=False,
    )
```

profile of v0, /device:TPU:0, one launch (start us, length us, event | category | flops | bytes accessed | tf_op | source)
XLA Modules:
  0.0 179.3 jit_solution(13614706876543647294)
XLA Ops:
  7.2 2.6 %copy.51 = bf16[128,4,1024]{2,0,1:T(8,128)(2,1)} copy(bf16[128,4,1024]{2,1,0:T(4,128)(2,1)} %param.11) | data formatting | bytes 2097152 | tf_op args[5]
  13.4 6.3 %all-to-all-start = ((bf16[8,16,4096]{2,1,0:T(8,128)(2,1)}), bf16[8,16,4096]{2,1,0:T(8,128)(2,1)S(1)}, u32[]{:S(2)}, u32[]{:S(2)}) async-start(bf16[8,16,4096]{2,1,0:T(8,128)(2,1)} %bitcast.2), calls=%async_computation | async-start | bytes 2097152 | tf_op jit(solution)/shard_map/all_to_all | solution.py:61
  19.8 2.1 %broadcast_in_dim.5 = f32[64,2,4096]{2,1,0:T(2,128)S(1)} broadcast(bf16[64,4096]{1,0:T(8,128)(2,1)} %param.7), dimensions={0,2} | broadcast | bytes 2621440 | tf_op jit(solution)/shard_map/broadcast_in_dim | solution.py:39
  21.9 2.4 %convert_element_type.97 = f32[128,4096]{1,0:T(8,128)} reshape(f32[64,2,4096]{2,1,0:T(2,128)S(1)} %broadcast_in_dim.5) | data formatting | bytes 4194304 | tf_op jit(solution)/shard_map/convert_element_type | solution.py:39
  24.6 3.1 %convolution_convert_fusion = bf16[128,4096]{1,0:T(8,128)(2,1)} fusion(f32[128,4096]{1,0:T(8,128)} %convert_element_type.97, f32[128]{0:T(128)S(1)} %mul.169, s32[128]{0:T(128)S(1)} %multiply_add_fusion.1), kind=kOutput, calls=%fused_computation.10 | convolution fusion | flops 135806976 | bytes 3146752 | tf_op jit(solution)/shard_map/dot_general | solution.py:44
  27.7 18.6 %all-to-all-done = bf16[8,16,4096]{2,1,0:T(8,128)(2,1)S(1)} async-done(((bf16[8,16,4096]{2,1,0:T(8,128)(2,1)}), bf16[8,16,4096]{2,1,0:T(8,128)(2,1)S(1)}, u32[]{:S(2)}, u32[]{:S(2)}) %all-to-all-start) | async-done | bytes 1048608 | tf_op jit(solution)/shard_map/all_to_all | solution.py:61
  46.3 4.2 %all-to-all-start.2 = ((bf16[8,16,4096]{2,1,0:T(8,128)(2,1)}), bf16[8,16,4096]{2,1,0:T(8,128)(2,1)}, u32[]{:S(2)}, u32[]{:S(2)}) async-start(bf16[8,16,4096]{2,1,0:T(8,128)(2,1)} %bitcast.16), calls=%async_computation.2 | async-start | bytes 2097152 | tf_op jit(solution)/shard_map/all_to_all | solution.py:62
  51.5 25.7 %all-to-all-done.2 = bf16[8,16,4096]{2,1,0:T(8,128)(2,1)} async-done(((bf16[8,16,4096]{2,1,0:T(8,128)(2,1)}), bf16[8,16,4096]{2,1,0:T(8,128)(2,1)}, u32[]{:S(2)}, u32[]{:S(2)}) %all-to-all-start.2) | async-done | bytes 1048608 | tf_op jit(solution)/shard_map/all_to_all | solution.py:62
  77.2 1.6 copy.66
  81.6 3.6 %fusion.2 = f32[4,32,8,1024]{3,2,1,0:T(8,128)S(1)} fusion(bf16[4,32,8,512]{3,2,1,0:T(8,128)(2,1)S(1)} %add_convert_fusion, bf16[512,4,1024]{2,0,1:T(8,128)(2,1)} %all-gather.2.cloned.1.call-done), kind=kOutput, calls=%fused_computation.14 | convolution fusion | flops 1073741824 | bytes 9437184 | tf_op jit(solution)/shard_map/erpc,ceo->erpo/dot_general | solution.py:72
  85.2 2.1 %multiply_convert_fusion.1 = (bf16[4,32,8,512]{3,2,1,0:T(8,128)(2,1)S(1)}, bf16[4,32,8,512]{3,2,1,0:T(8,128)(2,1)S(1)}, bf16[4,32,8,512]{3,2,1,0:T(8,128)(2,1)}) fusion(f32[4,32,8,512]{3,2,1,0:T(8,128)S(1)} %bitcast.82, f32[4,32,8,1024]{3,2,1,0:T(8,128)S(1)} %fusion.2), kind=kLoop, calls=%fused_computation.36 | loop fusion | flops 6291456 | bytes 9437184 | tf_op jit(solution)/shard_map/convert.16
  87.3 3.3 %bitcast_convert_fusion = bf16[4,1024,512]{2,1,0:T(8,128)(2,1)} fusion(bf16[4,32,8,512]{3,2,1,0:T(8,128)(2,1)S(1)} %add_convert_fusion, bf16[4,32,8,512]{3,2,1,0:T(8,128)(2,1)S(1)} %get-tuple-element.26, bf16[4,32,8,512]{3,2,1,0:T(8,128)(2,1)S(1)} %get-tuple-element.25), kind=kOutput, calls=%fused_computation | convolution fusion | flops 1080033280 | bytes 7340032 | tf_op jit(solution)/shard_map/erpc,erpo->ceo/dot_general | solution.py:96
  90.6 6.5 %copy.63 = bf16[512,4096]{1,0:T(8,128)(2,1)} copy(bf16[512,4096]{0,1:T(8,128)(2,1)} %bitcast.85) | data formatting | bytes 8388608
  98.3 3.8 %fusion = f32[4,32,8,512]{3,2,1,0:T(8,128)S(1)} fusion(bf16[512,4,1024]{2,0,1:T(8,128)(2,1)} %all-gather.2.cloned.1.call-done, bf16[4,32,8,512]{3,2,1,0:T(8,128)(2,1)} %copy-done.4, bf16[4,32,8,512]{3,2,1,0:T(8,128)(2,1)S(1)} %copy-done.3), kind=kOutput, calls=%fused_computation.12 | convolution fusion | flops 1077936128 | bytes 8388608 | tf_op jit(solution)/shard_map/erpo,ceo->erpc/dot_general | solution.py:82
  102.1 2.5 %multiply_reduce_fusion = (bf16[4,512]{1,0:T(4,128)(2,1)S(1)}, bf16[4,512]{1,0:T(4,128)(2,1)S(1)}, bf16[4,512]{1,0:T(4,128)(2,1)S(1)}, bf16[4,512]{1,0:T(4,128)(...) fusion(f32[4,32,8,512]{3,2,1,0:T(8,128)S(1)} %fusion, f32[4,32,8,512]{3,2,1,0:T(8,128)S(1)} %bitcast.79, ...), kind=kLoop, calls=%fused_computation.30 | loop fusion | flops 10475520 | bytes 5304320 | tf_op jit(solution)/shard_map/reduce_sum | solution.py:90
  106.1 1.6 copy.57
  107.6 3.8 %all-to-all-start.3 = ((bf16[8,16,4096]{2,1,0:T(8,128)(2,1)}), bf16[8,16,4096]{2,1,0:T(8,128)(2,1)S(1)}, u32[]{:S(2)}, u32[]{:S(2)}) async-start(bf16[8,16,4096]{2,1,0:T(8,128)(2,1)} %copy.57), calls=%async_computation.3 | async-start | bytes 2097152 | tf_op jit(solution)/shard_map/all_to_all | solution.py:105
  112.8 1.6 copy.53
  114.4 23.3 %all-to-all-done.3 = bf16[8,16,4096]{2,1,0:T(8,128)(2,1)S(1)} async-done(((bf16[8,16,4096]{2,1,0:T(8,128)(2,1)}), bf16[8,16,4096]{2,1,0:T(8,128)(2,1)S(1)}, u32[]{:S(2)}, u32[]{:S(2)}) %all-to-all-start.3) | async-done | bytes 1048608 | tf_op jit(solution)/shard_map/all_to_all | solution.py:105
  137.7 3.6 %all-to-all-start.1 = ((bf16[8,16,4096]{2,1,0:T(8,128)(2,1)}), bf16[8,16,4096]{2,1,0:T(8,128)(2,1)S(1)}, u32[]{:S(2)}, u32[]{:S(2)}) async-start(bf16[8,16,4096]{2,1,0:T(8,128)(2,1)} %copy.53), calls=%async_computation.1 | async-start | bytes 2097152 | tf_op jit(solution)/shard_map/all_to_all | solution.py:104
  141.6 16.2 %psum.7 = bf16[4,5,512]{2,0,1:T(4,128)(2,1)S(1)} all-reduce(bf16[4,5,512]{2,0,1:T(4,128)(2,1)S(1)} %constant_dynamic-update-slice_fusion), channel_id=1, replica_groups=mesh['dp'=4,'expert'=8] {'dp'}, use_global_device_ids=true, to_apply=%region_10.11 | all-reduce | flops 10240 | bytes 40960 | tf_op jit(solution)/shard_map/psum | solution.py:92
  159.7 8.1 %all-to-all-done.1 = bf16[8,16,4096]{2,1,0:T(8,128)(2,1)S(1)} async-done(((bf16[8,16,4096]{2,1,0:T(8,128)(2,1)}), bf16[8,16,4096]{2,1,0:T(8,128)(2,1)S(1)}, u32[]{:S(2)}, u32[]{:S(2)}) %all-to-all-start.1) | async-done | bytes 1048608 | tf_op jit(solution)/shard_map/all_to_all | solution.py:104
  169.1 1.6 copy.64
  170.7 1.8 copy.58
  (55 shorter events, 15.0 us)
Async XLA Ops:
  7.2 2.7 %copy-start.8 = (s32[64,2]{0,1:T(2,128)S(1)}, s32[64,2]{0,1:T(2,128)}, u32[]{:S(2)}) copy-start(s32[64,2]{0,1:T(2,128)} %param.8) | copy-start | bytes 1540
  7.2 2.9 %copy-start.5 = (bf16[64,4096]{1,0:T(8,128)(2,1)S(1)}, bf16[64,4096]{1,0:T(8,128)(2,1)}, u32[]{:S(2)}) copy-start(bf16[64,4096]{1,0:T(8,128)(2,1)} %param.6) | copy-start | bytes 1572868
  7.2 74.4 %all-gather.2.cloned.1.call-start = ((), (), s32[]{:S(2)}) async-start(), calls=%async_computation.5 | async-start | bytes 5242880 | tf_op jit(solution)/shard_map/all_gather | solution.py:71
  13.4 32.9 %all-to-all-start = ((bf16[8,16,4096]{2,1,0:T(8,128)(2,1)}), bf16[8,16,4096]{2,1,0:T(8,128)(2,1)S(1)}, u32[]{:S(2)}, u32[]{:S(2)}) async-start(bf16[8,16,4096]{2,1,0:T(8,128)(2,1)} %bitcast.2), calls=%async_computation | async-start | bytes 2097152 | tf_op jit(solution)/shard_map/all_to_all | solution.py:61
  21.9 2.5 %copy-start.7 = (f32[64,2]{0,1:T(2,128)S(1)}, f32[64,2]{0,1:T(2,128)}, u32[]{:S(2)}) copy-start(f32[64,2]{0,1:T(2,128)} %param.9) | copy-start | bytes 1540
  24.6 26.2 %copy-start.6 = (f32[4,5,512]{2,0,1:T(4,128)S(1)}, f32[4,5,512]{2,0,1:T(4,128)}, u32[]{:S(2)}) copy-start(f32[4,5,512]{2,0,1:T(4,128)} %param.10) | copy-start | bytes 122884
  46.3 30.8 %all-to-all-start.2 = ((bf16[8,16,4096]{2,1,0:T(8,128)(2,1)}), bf16[8,16,4096]{2,1,0:T(8,128)(2,1)}, u32[]{:S(2)}, u32[]{:S(2)}) async-start(bf16[8,16,4096]{2,1,0:T(8,128)(2,1)} %bitcast.16), calls=%async_computation.2 | async-start | bytes 2097152 | tf_op jit(solution)/shard_map/all_to_all | solution.py:62
  50.6 118.5 %reduce-scatter.4.cloned.1.call-start = ((), (), s32[]{:S(2)}) async-start(), calls=%async_computation.6 | async-start | bytes 5242880
  81.6 3.6 %copy-start = (f32[4,8,4,8,512]{4,3,2,1,0:T(8,128)S(1)}, f32[4,8,4,8,512]{4,3,2,1,0:T(8,128)}, u32[]{:S(2)}) copy-start(f32[4,8,4,8,512]{4,3,2,1,0:T(8,128)} %copy.55) | copy-start | bytes 6291460
  87.3 3.3 %copy-start.2 = (bf16[4,32,8,512]{3,2,1,0:T(8,128)(2,1)}, bf16[4,32,8,512]{3,2,1,0:T(8,128)(2,1)S(1)}, u32[]{:S(2)}) copy-start(bf16[4,32,8,512]{3,2,1,0:T(8,128)(2,1)S(1)} %get-tuple-element.25) | copy-start | bytes 3145732
  87.3 3.3 %copy-start.4 = (bf16[4,32,8,512]{3,2,1,0:T(8,128)(2,1)}, bf16[4,32,8,512]{3,2,1,0:T(8,128)(2,1)S(1)}, u32[]{:S(2)}) copy-start(bf16[4,32,8,512]{3,2,1,0:T(8,128)(2,1)S(1)} %get-tuple-element.26) | copy-start | bytes 3145732
  97.1 1.2 copy-start.3
  106.0 5.4 %copy-start.1 = (bf16[4,32,8,512]{3,2,1,0:T(8,128)(2,1)S(1)}, bf16[4,32,8,512]{3,2,1,0:T(8,128)(2,1)}, u32[]{:S(2)}) copy-start(bf16[4,32,8,512]{3,2,1,0:T(8,128)(2,1)} %get-tuple-element.27) | copy-start | bytes 3145732
  107.6 30.1 %all-to-all-start.3 = ((bf16[8,16,4096]{2,1,0:T(8,128)(2,1)}), bf16[8,16,4096]{2,1,0:T(8,128)(2,1)S(1)}, u32[]{:S(2)}, u32[]{:S(2)}) async-start(bf16[8,16,4096]{2,1,0:T(8,128)(2,1)} %copy.57), calls=%async_computation.3 | async-start | bytes 2097152 | tf_op jit(solution)/shard_map/all_to_all | solution.py:105
  137.7 30.1 %all-to-all-start.1 = ((bf16[8,16,4096]{2,1,0:T(8,128)(2,1)}), bf16[8,16,4096]{2,1,0:T(8,128)(2,1)S(1)}, u32[]{:S(2)}, u32[]{:S(2)}) async-start(bf16[8,16,4096]{2,1,0:T(8,128)(2,1)} %copy.53), calls=%async_computation.1 | async-start | bytes 2097152 | tf_op jit(solution)/shard_map/all_to_all | solution.py:104
Sparse Core Ops, SparseCore 0:
  9.9 55.3 all-gather.1
  97.2 51.7 reduce-scatter.3
where the time goes:
time: 180 us; the launch traced here: 179 us
  waiting for transfers between devices  75.8 us (42%)
  local copies, waits for them, and re-layouts  30.1 us (17%)
  starting transfers between devices  18.2 us (10%)
  matrix products  17.8 us (10%)
  blocking collectives  16.2 us (9%)
  between operations  14.3 us (8%)
  other arithmetic  6.93 us (4%)
    all_to_all x1, waiting for transfers between devices, shards(): lax.all_to_all(send_cotan, 'expert', split_axis=0, concat_axis=0, tiled=T...  25.7 us
    all_to_all x1, waiting for transfers between devices, shards(): lax.all_to_all(to_source(frame_grad), 'expert', split_axis=0, concat_axis...  23.3 us
    all_to_all x1, waiting for transfers between devices, shards(): lax.all_to_all(send_frames, 'expert', split_axis=0, concat_axis=0, tiled=...  18.6 us
    psum x1, blocking collectives, shards(): lax.psum(jnp.stack(tap_grads, axis=1).astype(jnp.bfloat16), 'dp')  16.2 us
    unnamed x30, local copies, waits for them, and re-layouts  15.9 us
    all_to_all x1, waiting for transfers between devices, shards(): lax.all_to_all(to_source(expert_out), 'expert', split_axis=0, concat_axis...  8.08 us
    all_to_all x1, starting transfers between devices, shards(): lax.all_to_all(send_frames, 'expert', split_axis=0, concat_axis=0, tiled=...  6.33 us
    all_to_all x1, starting transfers between devices, shards(): lax.all_to_all(send_cotan, 'expert', split_axis=0, concat_axis=0, tiled=T...  4.24 us
  transfers between devices with their start and end apart: 6, of which 4 were waited for; matrix products, arithmetic and copies ran while one was open for 18% of the time, Pallas kernels for 0%

commit v1 on v0

--- a/solution.py
+++ b/solution.py
@@ -6,6 +6,30 @@
 KERNEL_TAPS = 5
 DILATION_STEP = 2
 CAP = 4
+
+
+def cut_along(x, dim, size):
+    shape = x.shape
+    blocks = x.reshape(*shape[:dim], size, shape[dim] // size, *shape[dim + 1 :])
+    return jnp.moveaxis(blocks, dim, 0)
+
+
+def laid_out(parts, dim):
+    shape = list(parts.shape[1:])
+    shape[dim] *= parts.shape[0]
+    return jnp.moveaxis(parts, 0, dim).reshape(shape)
+
+
+def sent_to_each(value, axis, split_dim, concat_dim):
+    length, mine = (lax.axis_size(axis), lax.axis_index(axis))
+    parts = cut_along(value, split_dim, length)
+    filled = parts
+    for hop in range(1, length):
+        target, source = ((mine + hop) % length, (mine - hop) % length)
+        sent = lax.dynamic_index_in_dim(parts, target, 0)
+        theirs = lax.ppermute(sent, axis, [(i, (i + hop) % length) for i in range(length)])
+        filled = lax.dynamic_update_slice_in_dim(filled, theirs, source, axis=0)
+    return laid_out(filled, concat_dim)
 
 
 def shifted_input(field, tap_offset):
@@ -59,7 +83,7 @@
 
     recv_frames, recv_cotan = (
         lax.all_to_all(send_frames, "expert", split_axis=0, concat_axis=0, tiled=True),
-        lax.all_to_all(send_cotan, "expert", split_axis=0, concat_axis=0, tiled=True),
+        sent_to_each(send_cotan, "expert", 0, 0),
     )
     input_frames = to_local(recv_frames).astype(jnp.float32)
     hidden_state = jnp.zeros(input_frames.shape, jnp.float32)

time: 180 us -> 174 us (0.967)
  waiting for transfers between devices: 75.8 us -> 63.1 us
  starting transfers between devices: 18.2 us -> 28.3 us
  local copies, waits for them, and re-layouts: 30.1 us -> 27.9 us
    ppermute x0 -> x7, waiting for transfers between devices: none -> 31.3 us  [sent_to_each(): lax.ppermute(sent, axis, [(i, (i + hop) % length) for i in range(length)])]
    all_to_all x1 -> x0, waiting for transfers between devices: 25.7 us -> none  [shards(): lax.all_to_all(send_cotan, 'expert', split_axis=0, concat_axis=0, tiled=T...]
    all_to_all x1, waiting for transfers between devices: 18.6 us -> 0.01 us  [shards(): lax.all_to_all(send_frames, 'expert', split_axis=0, concat_axis=0, tiled=...]
    ppermute x0 -> x7, starting transfers between devices: none -> 8.5 us  [sent_to_each(): lax.ppermute(sent, axis, [(i, (i + hop) % length) for i in range(length)])]
    all_to_all x1, starting transfers between devices: 3.78 us -> 9.88 us  [shards(): lax.all_to_all(to_source(frame_grad), 'expert', split_axis=0, concat_axis...]
    all_to_all x1 -> x0, starting transfers between devices: 4.24 us -> none  [shards(): lax.all_to_all(send_cotan, 'expert', split_axis=0, concat_axis=0, tiled=T...]
    unnamed x30 -> x32, local copies, waits for them, and re-layouts: 15.9 us -> 14.7 us
  transfers between devices with their start and end apart: 6 -> 12, of which waited for: 4 -> 5; matrix products, arithmetic and copies ran while one was open for 18% -> 17% of each run, Pallas kernels for 0% -> 0%
where the time goes in v1:
time: 174 us
  waiting for transfers between devices  63.1 us (36%)
  starting transfers between devices  28.3 us (16%)
  local copies, waits for them, and re-layouts  27.9 us (16%)
  matrix products  16.8 us (10%)
  blocking collectives  16.2 us (9%)
  between operations  14.6 us (8%)
  other arithmetic  6.94 us (4%)
    ppermute x7, waiting for transfers between devices, sent_to_each(): lax.ppermute(sent, axis, [(i, (i + hop) % length) for i in range(length)])  31.3 us
    all_to_all x1, waiting for transfers between devices, shards(): lax.all_to_all(to_source(frame_grad), 'expert', split_axis=0, concat_axis...  23.6 us
    psum x1, blocking collectives, shards(): lax.psum(jnp.stack(tap_grads, axis=1).astype(jnp.bfloat16), 'dp')  16.2 us
    unnamed x32, local copies, waits for them, and re-layouts  14.7 us
    all_to_all x1, starting transfers between devices, shards(): lax.all_to_all(to_source(frame_grad), 'expert', split_axis=0, concat_axis...  9.88 us
    ppermute x7, starting transfers between devices, sent_to_each(): lax.ppermute(sent, axis, [(i, (i + hop) % length) for i in range(length)])  8.5 us
    all_to_all x1, waiting for transfers between devices, shards(): lax.all_to_all(to_source(expert_out), 'expert', split_axis=0, concat_axis...  8.06 us
    all_to_all x1, starting transfers between devices, shards(): lax.all_to_all(send_frames, 'expert', split_axis=0, concat_axis=0, tiled=...  6.29 us
  transfers between devices with their start and end apart: 12, of which 5 were waited for; matrix products, arithmetic and copies ran while one was open for 17% of the time, Pallas kernels for 0%

profile of v1, /device:TPU:0, one launch (start us, length us, event | category | flops | bytes accessed | tf_op | source)
XLA Modules:
  0.0 173.9 jit_solution(7581808371855673329)
XLA Ops:
  7.2 2.6 %copy.51 = bf16[128,4,1024]{2,0,1:T(8,128)(2,1)} copy(bf16[128,4,1024]{2,1,0:T(4,128)(2,1)} %param.11) | data formatting | bytes 2097152 | tf_op args[5]
  11.4 2.4 %convert_element_type.97 = f32[128,4096]{1,0:T(8,128)} reshape(f32[64,2,4096]{2,1,0:T(2,128)S(1)} %broadcast_in_dim.5) | data formatting | bytes 4194304 | tf_op jit(solution)/shard_map/convert_element_type | solution.py:63
  14.3 2.1 %convolution_convert_fusion = bf16[128,4096]{1,0:T(8,128)(2,1)S(1)} fusion(f32[128,4096]{1,0:T(8,128)} %convert_element_type.97, f32[128]{0:T(128)S(1)} %mul.169, s32[128]{0:T(128)S(1)} %multiply_add_fusion.1), kind=kOutput, calls=%fused_computation.10 | convolution fusion | flops 135806976 | bytes 3146752 | tf_op jit(solution)/shard_map/dot_general | solution.py:68
  19.8 6.3 %all-to-all-start = ((bf16[8,16,4096]{2,1,0:T(8,128)(2,1)}), bf16[8,16,4096]{2,1,0:T(8,128)(2,1)S(1)}, u32[]{:S(2)}, u32[]{:S(2)}) async-start(bf16[8,16,4096]{2,1,0:T(8,128)(2,1)} %bitcast.2), calls=%async_computation | async-start | bytes 2097152 | tf_op jit(solution)/shard_map/all_to_all | solution.py:85
  26.4 1.8 %collective-permute-start.1 = (bf16[1,1,16,4096]{3,2,0,1:T(8,128)(2,1)S(1)}, bf16[1,1,16,4096]{3,2,0,1:T(8,128)(2,1)S(1)}, u32[]{:S(2)}, u32[]{:S(2)}) collective-permute-start(bf16[1,1,16,4096]{3,2,0,1:T(8,128)(2,1)S(1)} %get-tuple-element.34), channel_id=1, source_target_pairs={{0,2},{1,3},{2,4},{3,5},{4,6},{5,7},{6,0},{7,1},{8,10},{9,11},{10,... | collective-permute-start | bytes 393224 | tf_op jit(solution)/shard_map/ppermute | solution.py:30
  30.7 2.3 %collective-permute-start.4 = (bf16[1,1,16,4096]{3,2,0,1:T(8,128)(2,1)S(1)}, bf16[1,1,16,4096]{3,2,0,1:T(8,128)(2,1)S(1)}, u32[]{:S(2)}, u32[]{:S(2)}) collective-permute-start(bf16[1,1,16,4096]{3,2,0,1:T(8,128)(2,1)S(1)} %get-tuple-element.31), channel_id=1, source_target_pairs={{0,5},{1,6},{2,7},{3,0},{4,1},{5,2},{6,3},{7,4},{8,13},{9,14},{10,... | collective-permute-start | bytes 393224 | tf_op jit(solution)/shard_map/ppermute | solution.py:30
  34.4 16.9 %collective-permute-done.1 = bf16[1,1,16,4096]{3,2,0,1:T(8,128)(2,1)S(1)} collective-permute-done((bf16[1,1,16,4096]{3,2,0,1:T(8,128)(2,1)S(1)}, bf16[1,1,16,4096]{3,2,0,1:T(8,128)(2,1)S(1)}, u32[]{:S(2)}, u32[]{:S(2)}) %collective-permute-start.1) | collective-permute-done | bytes 131104 | tf_op jit(solution)/shard_map/ppermute | solution.py:30
  51.4 13.4 %collective-permute-done.2 = bf16[1,1,16,4096]{3,2,0,1:T(8,128)(2,1)S(1)} collective-permute-done((bf16[1,1,16,4096]{3,2,0,1:T(8,128)(2,1)S(1)}, bf16[1,1,16,4096]{3,2,0,1:T(8,128)(2,1)S(1)}, u32[]{:S(2)}, u32[]{:S(2)}) %collective-permute-start.2) | collective-permute-done | bytes 131104 | tf_op jit(solution)/shard_map/ppermute | solution.py:30
  66.3 1.5 copy.55
  69.7 3.6 %fusion.2 = f32[4,32,8,1024]{3,2,1,0:T(8,128)S(1)} fusion(bf16[4,32,8,512]{3,2,1,0:T(8,128)(2,1)S(1)} %add_convert_fusion, bf16[512,4,1024]{2,0,1:T(8,128)(2,1)} %all-gather.2.cloned.1.call-done), kind=kOutput, calls=%fused_computation.14 | convolution fusion | flops 1073741824 | bytes 9437184 | tf_op jit(solution)/shard_map/erpc,ceo->erpo/dot_general | solution.py:96
  73.3 2.1 %multiply_convert_fusion.1 = (bf16[4,32,8,512]{3,2,1,0:T(8,128)(2,1)S(1)}, bf16[4,32,8,512]{3,2,1,0:T(8,128)(2,1)S(1)}, bf16[4,32,8,512]{3,2,1,0:T(8,128)(2,1)}) fusion(f32[4,32,8,512]{3,2,1,0:T(8,128)S(1)} %bitcast.87, f32[4,32,8,1024]{3,2,1,0:T(8,128)S(1)} %fusion.2), kind=kLoop, calls=%fused_computation.36 | loop fusion | flops 6291456 | bytes 9437184 | tf_op jit(solution)/shard_map/convert.16
  75.5 3.3 %bitcast_convert_fusion = bf16[4,1024,512]{2,1,0:T(8,128)(2,1)} fusion(bf16[4,32,8,512]{3,2,1,0:T(8,128)(2,1)S(1)} %add_convert_fusion, bf16[4,32,8,512]{3,2,1,0:T(8,128)(2,1)S(1)} %get-tuple-element.26, bf16[4,32,8,512]{3,2,1,0:T(8,128)(2,1)S(1)} %get-tuple-element.25), kind=kOutput, calls=%fused_computation | convolution fusion | flops 1080033280 | bytes 7340032 | tf_op jit(solution)/shard_map/erpc,erpo->ceo/dot_general | solution.py:120
  78.7 6.5 %copy.63 = bf16[512,4096]{1,0:T(8,128)(2,1)} copy(bf16[512,4096]{0,1:T(8,128)(2,1)} %bitcast.90) | data formatting | bytes 8388608
  86.4 3.8 %fusion = f32[4,32,8,512]{3,2,1,0:T(8,128)S(1)} fusion(bf16[512,4,1024]{2,0,1:T(8,128)(2,1)} %all-gather.2.cloned.1.call-done, bf16[4,32,8,512]{3,2,1,0:T(8,128)(2,1)} %copy-done.4, bf16[4,32,8,512]{3,2,1,0:T(8,128)(2,1)S(1)} %copy-done.3), kind=kOutput, calls=%fused_computation.12 | convolution fusion | flops 1077936128 | bytes 8388608 | tf_op jit(solution)/shard_map/erpo,ceo->erpc/dot_general | solution.py:106
  90.2 2.5 %multiply_reduce_fusion = (bf16[4,512]{1,0:T(4,128)(2,1)S(1)}, bf16[4,512]{1,0:T(4,128)(2,1)S(1)}, bf16[4,512]{1,0:T(4,128)(2,1)S(1)}, bf16[4,512]{1,0:T(4,128)(...) fusion(f32[4,32,8,512]{3,2,1,0:T(8,128)S(1)} %fusion, f32[4,32,8,512]{3,2,1,0:T(8,128)S(1)} %bitcast.81, ...), kind=kLoop, calls=%fused_computation.30 | loop fusion | flops 10475520 | bytes 5304320 | tf_op jit(solution)/shard_map/reduce_sum | solution.py:114
  94.2 1.6 copy.57
  95.8 9.9 %all-to-all-start.2 = ((bf16[8,16,4096]{2,1,0:T(8,128)(2,1)}), bf16[8,16,4096]{2,1,0:T(8,128)(2,1)S(1)}, u32[]{:S(2)}, u32[]{:S(2)}) async-start(bf16[8,16,4096]{2,1,0:T(8,128)(2,1)} %copy.57), calls=%async_computation.2 | async-start | bytes 2097152 | tf_op jit(solution)/shard_map/all_to_all | solution.py:129
  107.1 1.6 copy.53
  108.6 23.6 %all-to-all-done.2 = bf16[8,16,4096]{2,1,0:T(8,128)(2,1)S(1)} async-done(((bf16[8,16,4096]{2,1,0:T(8,128)(2,1)}), bf16[8,16,4096]{2,1,0:T(8,128)(2,1)S(1)}, u32[]{:S(2)}, u32[]{:S(2)}) %all-to-all-start.2) | async-done | bytes 1048608 | tf_op jit(solution)/shard_map/all_to_all | solution.py:129
  132.2 3.6 %all-to-all-start.1 = ((bf16[8,16,4096]{2,1,0:T(8,128)(2,1)}), bf16[8,16,4096]{2,1,0:T(8,128)(2,1)S(1)}, u32[]{:S(2)}, u32[]{:S(2)}) async-start(bf16[8,16,4096]{2,1,0:T(8,128)(2,1)} %copy.53), calls=%async_computation.1 | async-start | bytes 2097152 | tf_op jit(solution)/shard_map/all_to_all | solution.py:128
  136.1 16.2 %psum.7 = bf16[4,5,512]{2,0,1:T(4,128)(2,1)S(1)} all-reduce(bf16[4,5,512]{2,0,1:T(4,128)(2,1)S(1)} %constant_dynamic-update-slice_fusion), channel_id=1, replica_groups=mesh['dp'=4,'expert'=8] {'dp'}, use_global_device_ids=true, to_apply=%region_10.11 | all-reduce | flops 10240 | bytes 40960 | tf_op jit(solution)/shard_map/psum | solution.py:116
  154.3 8.1 %all-to-all-done.1 = bf16[8,16,4096]{2,1,0:T(8,128)(2,1)S(1)} async-done(((bf16[8,16,4096]{2,1,0:T(8,128)(2,1)}), bf16[8,16,4096]{2,1,0:T(8,128)(2,1)S(1)}, u32[]{:S(2)}, u32[]{:S(2)}) %all-to-all-start.1) | async-done | bytes 1048608 | tf_op jit(solution)/shard_map/all_to_all | solution.py:128
  163.6 1.6 copy.64
  165.3 1.8 %copy.58 = f32[128,4,1024]{2,1,0:T(4,128)} copy(bf16[128,4,1024]{0,2,1:T(8,128)(2,1)S(1)} %bitcast.89) | data formatting | bytes 3145728
  (77 shorter events, 20.2 us)
Async XLA Ops:
  7.2 2.7 %copy-start.9 = (s32[64,2]{0,1:T(2,128)S(1)}, s32[64,2]{0,1:T(2,128)}, u32[]{:S(2)}) copy-start(s32[64,2]{0,1:T(2,128)} %param.8) | copy-start | bytes 1540
  7.2 3.2 %copy-start.5 = (bf16[64,4096]{1,0:T(8,128)(2,1)S(1)}, bf16[64,4096]{1,0:T(8,128)(2,1)}, u32[]{:S(2)}) copy-start(bf16[64,4096]{1,0:T(8,128)(2,1)} %param.7) | copy-start | bytes 1572868
  7.2 62.5 %all-gather.2.cloned.1.call-start = ((), (), s32[]{:S(2)}) async-start(), calls=%async_computation.4 | async-start | bytes 5242880 | tf_op jit(solution)/shard_map/all_gather | solution.py:95
  11.4 2.5 %copy-start.8 = (f32[64,2]{0,1:T(2,128)S(1)}, f32[64,2]{0,1:T(2,128)}, u32[]{:S(2)}) copy-start(f32[64,2]{0,1:T(2,128)} %param.9) | copy-start | bytes 1540
  13.8 3.1 %copy-start.6 = (bf16[64,4096]{1,0:T(8,128)(2,1)S(1)}, bf16[64,4096]{1,0:T(8,128)(2,1)}, u32[]{:S(2)}) copy-start(bf16[64,4096]{1,0:T(8,128)(2,1)} %param.6) | copy-start | bytes 1572868
  16.4 10.0 %collective-permute-start = (bf16[1,1,16,4096]{3,2,0,1:T(8,128)(2,1)S(1)}, bf16[1,1,16,4096]{3,2,0,1:T(8,128)(2,1)S(1)}, u32[]{:S(2)}, u32[]{:S(2)}) collective-permute-start(bf16[1,1,16,4096]{3,2,0,1:T(8,128)(2,1)S(1)} %constant_dynamic-slice_fusion.6), channel_id=1, source_target_pairs={{0,1},{1,2},{2,3},{3,4},{4,5},{5,6},{6,7},{7,0},{8,9},{9,10},{10,1... | collective-permute-start | bytes 393224 | tf_op jit(solution)/shard_map/ppermute | solution.py:30
  19.8 8.5 %copy-start.7 = (f32[4,5,512]{2,0,1:T(4,128)S(1)}, f32[4,5,512]{2,0,1:T(4,128)}, u32[]{:S(2)}) copy-start(f32[4,5,512]{2,0,1:T(4,128)} %param.10) | copy-start | bytes 122884
  19.8 48.1 %all-to-all-start = ((bf16[8,16,4096]{2,1,0:T(8,128)(2,1)}), bf16[8,16,4096]{2,1,0:T(8,128)(2,1)S(1)}, u32[]{:S(2)}, u32[]{:S(2)}) async-start(bf16[8,16,4096]{2,1,0:T(8,128)(2,1)} %bitcast.2), calls=%async_computation | async-start | bytes 2097152 | tf_op jit(solution)/shard_map/all_to_all | solution.py:85
  26.1 137.6 %reduce-scatter.4.cloned.1.call-start = ((), (), s32[]{:S(2)}) async-start(), calls=%async_computation.5 | async-start | bytes 5242880
  26.4 24.9 %collective-permute-start.1 = (bf16[1,1,16,4096]{3,2,0,1:T(8,128)(2,1)S(1)}, bf16[1,1,16,4096]{3,2,0,1:T(8,128)(2,1)S(1)}, u32[]{:S(2)}, u32[]{:S(2)}) collective-permute-start(bf16[1,1,16,4096]{3,2,0,1:T(8,128)(2,1)S(1)} %get-tuple-element.34), channel_id=1, source_target_pairs={{0,2},{1,3},{2,4},{3,5},{4,6},{5,7},{6,0},{7,1},{8,10},{9,11},{10,... | collective-permute-start | bytes 393224 | tf_op jit(solution)/shard_map/ppermute | solution.py:30
  28.3 36.6 %collective-permute-start.2 = (bf16[1,1,16,4096]{3,2,0,1:T(8,128)(2,1)S(1)}, bf16[1,1,16,4096]{3,2,0,1:T(8,128)(2,1)S(1)}, u32[]{:S(2)}, u32[]{:S(2)}) collective-permute-start(bf16[1,1,16,4096]{3,2,0,1:T(8,128)(2,1)S(1)} %get-tuple-element.33), channel_id=1, source_target_pairs={{0,3},{1,4},{2,5},{3,6},{4,7},{5,0},{6,1},{7,2},{8,11},{9,12},{10,... | collective-permute-start | bytes 393224 | tf_op jit(solution)/shard_map/ppermute | solution.py:30
  29.2 36.6 %collective-permute-start.3 = (bf16[1,1,16,4096]{3,2,0,1:T(8,128)(2,1)S(1)}, bf16[1,1,16,4096]{3,2,0,1:T(8,128)(2,1)S(1)}, u32[]{:S(2)}, u32[]{:S(2)}) collective-permute-start(bf16[1,1,16,4096]{3,2,0,1:T(8,128)(2,1)S(1)} %get-tuple-element.32), channel_id=1, source_target_pairs={{0,4},{1,5},{2,6},{3,7},{4,0},{5,1},{6,2},{7,3},{8,12},{9,13},{10,... | collective-permute-start | bytes 393224 | tf_op jit(solution)/shard_map/ppermute | solution.py:30
  30.7 35.1 %collective-permute-start.4 = (bf16[1,1,16,4096]{3,2,0,1:T(8,128)(2,1)S(1)}, bf16[1,1,16,4096]{3,2,0,1:T(8,128)(2,1)S(1)}, u32[]{:S(2)}, u32[]{:S(2)}) collective-permute-start(bf16[1,1,16,4096]{3,2,0,1:T(8,128)(2,1)S(1)} %get-tuple-element.31), channel_id=1, source_target_pairs={{0,5},{1,6},{2,7},{3,0},{4,1},{5,2},{6,3},{7,4},{8,13},{9,14},{10,... | collective-permute-start | bytes 393224 | tf_op jit(solution)/shard_map/ppermute | solution.py:30
  33.0 32.9 %collective-permute-start.5 = (bf16[1,1,16,4096]{3,2,0,1:T(8,128)(2,1)S(1)}, bf16[1,1,16,4096]{3,2,0,1:T(8,128)(2,1)S(1)}, u32[]{:S(2)}, u32[]{:S(2)}) collective-permute-start(bf16[1,1,16,4096]{3,2,0,1:T(8,128)(2,1)S(1)} %get-tuple-element.30), channel_id=1, source_target_pairs={{0,6},{1,7},{2,0},{3,1},{4,2},{5,3},{6,4},{7,5},{8,14},{9,15},{10,... | collective-permute-start | bytes 393224 | tf_op jit(solution)/shard_map/ppermute | solution.py:30
  51.4 14.5 %collective-permute-start.6 = (bf16[1,1,16,4096]{3,2,0,1:T(8,128)(2,1)S(1)}, bf16[1,1,16,4096]{3,2,0,1:T(8,128)(2,1)S(1)}, u32[]{:S(2)}, u32[]{:S(2)}) collective-permute-start(bf16[1,1,16,4096]{3,2,0,1:T(8,128)(2,1)S(1)} %get-tuple-element.29), channel_id=1, source_target_pairs={{0,7},{1,0},{2,1},{3,2},{4,3},{5,4},{6,5},{7,6},{8,15},{9,8},{10,9... | collective-permute-start | bytes 393224 | tf_op jit(solution)/shard_map/ppermute | solution.py:30
  69.7 3.6 %copy-start = (f32[4,8,4,8,512]{4,3,2,1,0:T(8,128)S(1)}, f32[4,8,4,8,512]{4,3,2,1,0:T(8,128)}, u32[]{:S(2)}) copy-start(f32[4,8,4,8,512]{4,3,2,1,0:T(8,128)} %copy.55) | copy-start | bytes 6291460
  75.5 3.3 %copy-start.2 = (bf16[4,32,8,512]{3,2,1,0:T(8,128)(2,1)}, bf16[4,32,8,512]{3,2,1,0:T(8,128)(2,1)S(1)}, u32[]{:S(2)}) copy-start(bf16[4,32,8,512]{3,2,1,0:T(8,128)(2,1)S(1)} %get-tuple-element.25) | copy-start | bytes 3145732
  75.5 3.3 %copy-start.4 = (bf16[4,32,8,512]{3,2,1,0:T(8,128)(2,1)}, bf16[4,32,8,512]{3,2,1,0:T(8,128)(2,1)S(1)}, u32[]{:S(2)}) copy-start(bf16[4,32,8,512]{3,2,1,0:T(8,128)(2,1)S(1)} %get-tuple-element.26) | copy-start | bytes 3145732
  85.2 1.2 copy-start.3
  94.2 11.5 %copy-start.1 = (bf16[4,32,8,512]{3,2,1,0:T(8,128)(2,1)S(1)}, bf16[4,32,8,512]{3,2,1,0:T(8,128)(2,1)}, u32[]{:S(2)}) copy-start(bf16[4,32,8,512]{3,2,1,0:T(8,128)(2,1)} %get-tuple-element.27) | copy-start | bytes 3145732
  95.8 36.5 %all-to-all-start.2 = ((bf16[8,16,4096]{2,1,0:T(8,128)(2,1)}), bf16[8,16,4096]{2,1,0:T(8,128)(2,1)S(1)}, u32[]{:S(2)}, u32[]{:S(2)}) async-start(bf16[8,16,4096]{2,1,0:T(8,128)(2,1)} %copy.57), calls=%async_computation.2 | async-start | bytes 2097152 | tf_op jit(solution)/shard_map/all_to_all | solution.py:129
  132.2 30.1 %all-to-all-start.1 = ((bf16[8,16,4096]{2,1,0:T(8,128)(2,1)}), bf16[8,16,4096]{2,1,0:T(8,128)(2,1)S(1)}, u32[]{:S(2)}, u32[]{:S(2)}) async-start(bf16[8,16,4096]{2,1,0:T(8,128)(2,1)} %copy.53), calls=%async_computation.1 | async-start | bytes 2097152 | tf_op jit(solution)/shard_map/all_to_all | solution.py:128
Sparse Core Ops, SparseCore 0:
  9.9 55.3 all-gather.1
  85.4 59.2 reduce-scatter.3
